TPU v7x, 256 devices: a whole 4x4x8 slice. The times are simulated.
256 devices in a mesh: wide: 16 (over z_lo, x, core), long: 16 (over y, z_hi).
Axes of the slice: x: 4, y: 4, z: 8 (z_hi: 4, z_lo: 2; z = z_hi * 2 + z_lo), core: 2. Of those that a mesh axis runs over, the one named last changes fastest.
Arguments:
- slab_vertices: float32 [3, 4096], P(None, 'wide'), may hold values from 0 to 1
- slab_elements: int32 [3, 8192], P(None, 'wide'), may hold values from 0 to 4095, as said below
- source_vertices: float32 [3, 16384], P(None, ('wide', 'long')), may hold values from 0 to 1
- source_elements: int32 [3, 32768], P(None, ('wide', 'long')), may hold values from 0 to 16383, as said below
- primal_basis: bfloat16 [32, 32768], P(None, ('wide', 'long')), may hold values from -12 to 12
- adjoint_basis: bfloat16 [32, 8192], P(None, 'wide'), may hold values from -24 to 24
Outputs:
- primal_image: float32 [32, 8192], P(None, ('wide', 'long'))
- adjoint_image: float32 [32, 32768], P(None, ('wide', 'long'))
Inputs may be any that keep to these rules, and one draw needn't show every extreme that they name: `slab_elements`: a slab triangle in columns b * 512 to (b + 1) * 512 - 1 names only vertices b * 256 to (b + 1) * 256 - 1; both ends of each such range are named. `source_elements`: a source triangle in columns b * 128 to (b + 1) * 128 - 1 names only vertices b * 64 to (b + 1) * 64 - 1; both ends of each such range are named.
All inputs are finite; a program needn't handle non-finite values.
Results may differ from a plain program's by a relative error of at most 0.0029.
Values may be sent and summed in bfloat16 or wider, within the bound.
A program may use at most 64 MiB of HBM per device.

v0:
```python
import math
import jax
import jax.numpy as jnp
from jax import lax
from jax.sharding import PartitionSpec as P

WAVENUMBER = 40.0
SOFTENING = 0.0004
AREA_WEIGHT = 0.05
FOUR_PI = 4.0 * math.pi


def geometry(vertices, elements, anchor):
    local_ids = elements - anchor
    corners = [jnp.take(vertices, local_ids[corner], axis=1) for corner in range(3)]
    centre = (corners[0] + corners[1] + corners[2]) / 3.0
    edge_one = corners[1] - corners[0]
    edge_two = corners[2] - corners[0]
    normal_x = edge_one[1] * edge_two[2] - edge_one[2] * edge_two[1]
    normal_y = edge_one[2] * edge_two[0] - edge_one[0] * edge_two[2]
    normal_z = edge_one[0] * edge_two[1] - edge_one[1] * edge_two[0]
    areas = 0.5 * jnp.sqrt(normal_x * normal_x + normal_y * normal_y + normal_z * normal_z)
    return jnp.concatenate([centre, areas[None, :]], axis=0)


def kernel_tile(targets, sources):
    spread = targets[0][:, None] - sources[0][None, :]
    square_sum = spread * spread
    for axis_id in range(1, 3):
        spread = targets[axis_id][:, None] - sources[axis_id][None, :]
        square_sum = square_sum + spread * spread
    radius = jnp.sqrt(
        square_sum + SOFTENING + AREA_WEIGHT * (targets[3][:, None] + sources[3][None, :])
    )
    weight = targets[3][:, None] * sources[3][None, :] / (FOUR_PI * radius)
    phases = WAVENUMBER * radius
    return (
        (weight * jnp.cos(phases)).astype(jnp.bfloat16),
        (weight * jnp.sin(phases)).astype(jnp.bfloat16),
    )


def pack_primal(columns):
    half_rows = columns.shape[0] // 2
    real_part = columns[:half_rows]
    imag_part = columns[half_rows:]
    return jnp.concatenate(
        [jnp.concatenate([real_part, -imag_part], 1), jnp.concatenate([imag_part, real_part], 1)], 0
    )


def pack_adjoint(row_block):
    half_rows = row_block.shape[0] // 2
    real_part = row_block[:half_rows]
    imag_part = row_block[half_rows:]
    return jnp.concatenate(
        [jnp.concatenate([real_part, imag_part], 1), jnp.concatenate([imag_part, -real_part], 1)], 0
    )


def primal_part(primal_pack, tile_real, tile_imag):
    stacked = jnp.concatenate([tile_real, tile_imag], 1)
    return lax.dot_general(
        primal_pack, stacked, (((1,), (1,)), ((), ())), preferred_element_type=jnp.float32
    )


def adjoint_part(adjoint_pack, tile_real, tile_imag):
    stacked = jnp.concatenate([tile_real, tile_imag], 0)
    return jnp.dot(adjoint_pack, stacked, preferred_element_type=jnp.float32)


def shards(
    slab_vertices, slab_elements, source_vertices, source_elements, primal_basis, adjoint_basis
):
    slab_width = slab_elements.shape[1]
    source_width = source_elements.shape[1]
    wide_at = lax.axis_index("wide")
    flat_at = wide_at * lax.axis_size("long") + lax.axis_index("long")
    slab_points = geometry(slab_vertices, slab_elements, wide_at * (slab_width // 2))
    source_points = geometry(source_vertices, source_elements, flat_at * (source_width // 2))
    gathered_points = lax.all_gather(source_points, "wide", axis=1, tiled=True)
    gathered_basis = lax.all_gather(primal_basis, "wide", axis=1, tiled=True)
    tile_real, tile_imag = kernel_tile(slab_points, gathered_points)
    primal_acc = primal_part(pack_primal(gathered_basis), tile_real, tile_imag)
    adjoint_acc = adjoint_part(pack_adjoint(adjoint_basis), tile_real, tile_imag)
    primal_image = lax.psum_scatter(primal_acc, "long", scatter_dimension=1, tiled=True)
    adjoint_image = lax.psum_scatter(adjoint_acc, "wide", scatter_dimension=1, tiled=True)
    return (primal_image, adjoint_image)


def solution(mesh):
    return jax.shard_map(
        shards,
        mesh=mesh,
        in_specs=(
            P(None, "wide"),
            P(None, "wide"),
            P(None, ("wide", "long")),
            P(None, ("wide", "long")),
            P(None, ("wide", "long")),
            P(None, "wide"),
        ),
        out_specs=(P(None, ("wide", "long")), P(None, ("wide", "long"))),
        check_vma=False,
    )
```

profile of v0, /device:TPU:8, one launch (start us, length us, event | category | flops | bytes accessed | tf_op | source)
XLA Modules:
  0.0 232.3 jit_solution(14007705249488354865)
XLA Ops:
  7.2 0.0 reduce-scatter.7.cloned.1.call-start
  7.2 0.7 broadcast_subtract_fusion
  8.0 0.8 copy.35
  8.8 0.7 broadcast_subtract_fusion.1
  9.5 0.6 gather_fusion.5
  10.1 0.1 copy.40
  10.2 0.7 gather_fusion.4
  10.9 0.1 copy.38
  10.9 0.7 gather_fusion.3
  11.6 0.1 copy.36
  11.7 20.1 %all_gather.7 = f32[4,2048]{1,0:T(4,128)S(1)} all-gather(f32[4,128]{1,0:T(4,128)S(1)} %pad_maximum_fusion), channel_id=1, replica_groups=mesh['wide'=16,'long'=16] {'wide'}, dimensions={1}, use_global_device_ids=true | all-gather | bytes 34816 | tf_op jit(solution)/shard_map/all_gather | solution.py:82
  31.8 0.8 copy.29
  32.7 1.0 gather_fusion.2
  33.7 0.1 copy.34
  33.8 1.0 gather_fusion.1
  34.9 0.1 copy.32
  35.0 1.0 gather_fusion
  36.1 0.1 copy.30
  36.2 16.9 %all_gather.6 = bf16[32,2048]{1,0:T(8,128)(2,1)S(1)} all-gather(bf16[32,128]{1,0:T(8,128)(2,1)} %param.14), channel_id=1, replica_groups=mesh['wide'=16,'long'=16] {'wide'}, dimensions={1}, use_global_device_ids=true | all-gather | bytes 139264 | tf_op jit(solution)/shard_map/all_gather | solution.py:83
  53.1 19.3 %multiply_convert_fusion.1 = (bf16[512,2048]{1,0:T(8,128)(2,1)S(1)}, bf16[512,2048]{1,0:T(8,128)(2,1)S(1)}) fusion(f32[2048]{0:T(1024)S(1)} %bitcast.59, f32[512]{0:T(512)S(1)} %bitcast.64, f32[2048]{0:T(1024)S(1)} %bitcast.60, f32[512]{0:T(512)S(1)} %bitcast.65, f32[2048]{0:T(1024)S(1)} %bitcast.61, f32[512]{0:T(512)S(1)} %bitcast.63, ...), kind=kLoop, calls=%fused_computation.15 | loop fusion | flops 20971520 | bytes 4235264 | tf_op jit(solution)/shard_map/convert_element_type | solution.py:38
  72.4 0.0 copy-start.1
  72.4 1.3 copy-done.1
  73.7 0.0 copy-start
  73.7 1.9 fusion.8
  75.6 0.0 reduce-scatter.7.cloned.1.call-update
  75.6 0.0 reduce-scatter.5.cloned.1.call-start
  75.7 0.0 copy-done
  75.7 3.1 %fusion.4 = f32[32,2048]{1,0:T(8,128)} fusion(bf16[512,2048]{1,0:T(8,128)(2,1)} %copy-done.1, bf16[512,2048]{1,0:T(8,128)(2,1)S(1)} %get-tuple-element.13, bf16[16,512]{1,0:T(8,128)(2,1)S(1)} %get-tuple-element.16, bf16[16,512]{1,0:T(8,128)(2,1)S(1)} %get-tuple-element.17, bf16[16,512]{1,0:T(8,128)(2,1)S(1)} %get-tuple-element.15), kind=kOutput, calls=%fused_computation.10 | convolution fusion | flops 142868480 | bytes 4505600 | tf_op jit(solution)/shard_map/dot_general | solution.py:70
  78.8 0.0 reduce-scatter.5.cloned.1.call-update
  78.9 82.1 %reduce-scatter.7.cloned.1.call-done = f32[32,32]{1,0:T(8,128)} async-done(((f32[512,32]{1,0:T(8,128)}), f32[32,32]{1,0:T(8,128)}) %reduce-scatter.7.cloned.1.call-update) | async-done | bytes 4112
  161.0 1.4 copy.42
  162.3 63.1 %reduce-scatter.5.cloned.1.call-done = f32[32,128]{1,0:T(8,128)} async-done(((f32[32,2048]{1,0:T(8,128)}), f32[32,128]{1,0:T(8,128)}) %reduce-scatter.5.cloned.1.call-update) | async-done | bytes 16400 | tf_op jit(solution)/shard_map/reduce_scatter | solution.py:88
  (21 shorter events, 0.2 us)
Async XLA Ops:
  7.2 153.8 %reduce-scatter.7.cloned.1.call-start = ((), (), s32[]{:S(2)}) async-start(), calls=%async_computation.3 | async-start | bytes 278528
  72.4 1.3 copy-start.1
  73.7 2.0 copy-start
  75.6 149.8 %reduce-scatter.5.cloned.1.call-start = ((), (), s32[]{:S(2)}) async-start(), calls=%async_computation.2 | async-start | bytes 278528 | tf_op jit(solution)/shard_map/reduce_scatter | solution.py:88
Sparse Core Ops, SparseCore 0:
  75.8 85.1 reduce-scatter.6
  164.2 61.2 reduce-scatter.4
where the time goes:
time: 233 us; the launch traced here: 232 us
  waiting for transfers between devices  145 us (62%)
  blocking collectives  37 us (16%)
  other arithmetic  20.8 us (9%)
  between operations  14.2 us (6%)
  local copies, waits for them, and re-layouts  9.95 us (4%)
  matrix products  5.05 us (2%)
    unnamed x3, waiting for transfers between devices  82.1 us
    reduce_scatter x1, waiting for transfers between devices, shards(): lax.psum_scatter(adjoint_acc, 'wide', scatter_dimension=1, tiled=True)  63.1 us
    all_gather x1, blocking collectives, shards(): gathered_points = lax.all_gather(source_points, 'wide', axis=1, tiled=True)  20.1 us
    convert_element_type x1, other arithmetic, kernel_tile(): (weight * jnp.cos(phases)).astype(jnp.bfloat16)  19.3 us
    all_gather x1, blocking collectives, shards(): gathered_basis = lax.all_gather(primal_basis, 'wide', axis=1, tiled=True)  16.9 us
    gather x12, local copies, waits for them, and re-layouts, geometry(): jnp.take(vertices, local_ids[corner], axis=1)  5.6 us
  transfers between devices with their start and end apart: 2, of which 2 were waited for; matrix products, arithmetic and copies ran while one was open for 2% of the time, Pallas kernels for 0%

commit v1 on v0

--- a/solution.py
+++ b/solution.py
@@ -79,7 +79,10 @@
     flat_at = wide_at * lax.axis_size("long") + lax.axis_index("long")
     slab_points = geometry(slab_vertices, slab_elements, wide_at * (slab_width // 2))
     source_points = geometry(source_vertices, source_elements, flat_at * (source_width // 2))
-    gathered_points = lax.all_gather(source_points, "wide", axis=1, tiled=True)
+    size = lax.axis_size("wide")
+    pieces = jnp.stack([source_points for _ in range(size)])
+    pieces = lax.all_to_all(pieces, "wide", split_axis=0, concat_axis=0)
+    gathered_points = jnp.concatenate(pieces, axis=1)
     gathered_basis = lax.all_gather(primal_basis, "wide", axis=1, tiled=True)
     tile_real, tile_imag = kernel_tile(slab_points, gathered_points)
     primal_acc = primal_part(pack_primal(gathered_basis), tile_real, tile_imag)

time: 233 us -> 222 us (0.953)
  blocking collectives: 37 us -> 20.5 us
  starting transfers between devices: 0.08 us -> 5.84 us
    all_gather x1 -> x0, blocking collectives: 20.1 us -> none  [shards(): gathered_points = lax.all_gather(source_points, 'wide', axis=1, tiled=True)]
    all_to_all x0 -> x1, starting transfers between devices: none -> 5.76 us  [shards(): pieces = lax.all_to_all(pieces, 'wide', split_axis=0, concat_axis=0)]
    all_gather x1, blocking collectives: 16.9 us -> 20.5 us  [shards(): gathered_basis = lax.all_gather(primal_basis, 'wide', axis=1, tiled=True)]
  transfers between devices with their start and end apart: 2 -> 3, of which waited for: 2 -> 2; matrix products, arithmetic and copies ran while one was open for 2% -> 4% of each run, Pallas kernels for 0% -> 0%
where the time goes in v1:
time: 222 us; the launch traced here: 221 us
  waiting for transfers between devices  144 us (65%)
  other arithmetic  20.8 us (9%)
  blocking collectives  20.5 us (9%)
  between operations  14.2 us (6%)
  local copies, waits for them, and re-layouts  10.6 us (5%)
  starting transfers between devices  5.84 us (3%)
  matrix products  5.07 us (2%)
    unnamed x3, waiting for transfers between devices  81.2 us
    reduce_scatter x1, waiting for transfers between devices, shards(): lax.psum_scatter(adjoint_acc, 'wide', scatter_dimension=1, tiled=True)  62.9 us
    all_gather x1, blocking collectives, shards(): gathered_basis = lax.all_gather(primal_basis, 'wide', axis=1, tiled=True)  20.5 us
    convert_element_type x1, other arithmetic, kernel_tile(): (weight * jnp.cos(phases)).astype(jnp.bfloat16)  19.3 us
    all_to_all x1, starting transfers between devices, shards(): pieces = lax.all_to_all(pieces, 'wide', split_axis=0, concat_axis=0)  5.76 us
    gather x12, local copies, waits for them, and re-layouts, geometry(): jnp.take(vertices, local_ids[corner], axis=1)  5.6 us
  transfers between devices with their start and end apart: 3, of which 2 were waited for; matrix products, arithmetic and copies ran while one was open for 4% of the time, Pallas kernels for 0%

profile of v1, /device:TPU:8, one launch (start us, length us, event | category | flops | bytes accessed | tf_op | source)
XLA Modules:
  0.0 221.1 jit_solution(3437253569537557720)
XLA Ops:
  7.2 0.0 copy-start
  7.2 0.8 copy.37
  8.0 0.7 broadcast_subtract_fusion.1
  8.7 0.6 gather_fusion.5
  9.3 0.1 copy.42
  9.4 0.7 gather_fusion.4
  10.0 0.1 copy.40
  10.1 0.7 gather_fusion.3
  10.8 0.1 copy.38
  10.9 0.6 stack.2
  11.5 5.8 %all-to-all-start = ((f32[16,4,128]{2,1,0:T(4,128)}), f32[16,4,128]{2,1,0:T(4,128)S(1)}, u32[]{:S(2)}, u32[]{:S(2)}) async-start(f32[16,4,128]{2,1,0:T(4,128)} %stack.2), calls=%async_computation | async-start | bytes 65536 | tf_op jit(solution)/shard_map/all_to_all | solution.py:84
  17.3 0.0 reduce-scatter.7.cloned.1.call-start
  17.3 0.7 broadcast_subtract_fusion
  18.1 0.8 copy.31
  19.0 1.0 gather_fusion.2
  20.0 0.1 copy.36
  20.1 1.0 gather_fusion.1
  21.2 0.1 copy.34
  21.3 1.0 gather_fusion
  22.3 0.1 copy.32
  22.4 20.5 %all_gather.3 = bf16[32,2048]{1,0:T(8,128)(2,1)S(1)} all-gather(bf16[32,128]{1,0:T(8,128)(2,1)} %param.14), channel_id=1, replica_groups=mesh['wide'=16,'long'=16] {'wide'}, dimensions={1}, use_global_device_ids=true | all-gather | bytes 139264 | tf_op jit(solution)/shard_map/all_gather | solution.py:86
  43.0 0.0 copy-done
  43.1 0.0 all-to-all-done
  43.1 19.3 %multiply_convert_fusion.1 = (bf16[512,2048]{1,0:T(8,128)(2,1)S(1)}, bf16[512,2048]{1,0:T(8,128)(2,1)S(1)}) fusion(f32[2048]{0:T(1024)S(1)} %bitcast.61, f32[512]{0:T(512)S(1)} %bitcast.65, f32[2048]{0:T(1024)S(1)} %bitcast.62, f32[512]{0:T(512)S(1)} %bitcast.66, f32[2048]{0:T(1024)S(1)} %bitcast.63, f32[512]{0:T(512)S(1)} %bitcast.64, ...), kind=kLoop, calls=%fused_computation.15 | loop fusion | flops 20971520 | bytes 4235264 | tf_op jit(solution)/shard_map/convert_element_type | solution.py:38
  62.4 0.0 copy-start.1
  62.4 1.3 copy-done.1
  63.7 1.9 fusion.8
  65.7 0.0 reduce-scatter.7.cloned.1.call-update
  65.7 0.0 reduce-scatter.5.cloned.1.call-start
  65.8 3.1 %fusion.4 = f32[32,2048]{1,0:T(8,128)} fusion(bf16[512,2048]{1,0:T(8,128)(2,1)} %copy-done.1, bf16[512,2048]{1,0:T(8,128)(2,1)S(1)} %get-tuple-element.13, bf16[16,512]{1,0:T(8,128)(2,1)S(1)} %get-tuple-element.16, bf16[16,512]{1,0:T(8,128)(2,1)S(1)} %get-tuple-element.17, bf16[16,512]{1,0:T(8,128)(2,1)S(1)} %get-tuple-element.15), kind=kOutput, calls=%fused_computation.10 | convolution fusion | flops 142868480 | bytes 4505600 | tf_op jit(solution)/shard_map/dot_general | solution.py:70
  68.9 0.0 reduce-scatter.5.cloned.1.call-update
  68.9 81.1 %reduce-scatter.7.cloned.1.call-done = f32[32,32]{1,0:T(8,128)} async-done(((f32[512,32]{1,0:T(8,128)}), f32[32,32]{1,0:T(8,128)}) %reduce-scatter.7.cloned.1.call-update) | async-done | bytes 4112
  150.0 1.4 copy.44
  151.4 62.9 %reduce-scatter.5.cloned.1.call-done = f32[32,128]{1,0:T(8,128)} async-done(((f32[32,2048]{1,0:T(8,128)}), f32[32,128]{1,0:T(8,128)}) %reduce-scatter.5.cloned.1.call-update) | async-done | bytes 16400 | tf_op jit(solution)/shard_map/reduce_scatter | solution.py:91
  (21 shorter events, 0.2 us)
Async XLA Ops:
  7.2 35.8 %copy-start = (bf16[32,512]{1,0:T(8,128)(2,1)S(1)}, bf16[32,512]{1,0:T(8,128)(2,1)}, u32[]{:S(2)}) copy-start(bf16[32,512]{1,0:T(8,128)(2,1)} %param.15) | copy-start | bytes 98308
  11.5 31.6 %all-to-all-start = ((f32[16,4,128]{2,1,0:T(4,128)}), f32[16,4,128]{2,1,0:T(4,128)S(1)}, u32[]{:S(2)}, u32[]{:S(2)}) async-start(f32[16,4,128]{2,1,0:T(4,128)} %stack.2), calls=%async_computation | async-start | bytes 65536 | tf_op jit(solution)/shard_map/all_to_all | solution.py:84
  17.3 132.8 %reduce-scatter.7.cloned.1.call-start = ((), (), s32[]{:S(2)}) async-start(), calls=%async_computation.4 | async-start | bytes 278528
  62.4 1.3 copy-start.1
  65.7 148.6 %reduce-scatter.5.cloned.1.call-start = ((), (), s32[]{:S(2)}) async-start(), calls=%async_computation.3 | async-start | bytes 278528 | tf_op jit(solution)/shard_map/reduce_scatter | solution.py:91
Sparse Core Ops, SparseCore 0:
  65.8 84.1 reduce-scatter.6
  153.2 61.0 reduce-scatter.4
